TPU v7x, 32 devices: a whole 2x2x4 slice. The times are simulated.
32 devices in a mesh: group: 2 (over y), gx: 4 (over z), gy: 2 (over x), gz: 2 (over core).
Axes of the slice: x: 2, y: 2, z: 4, core: 2. Of those that a mesh axis runs over, the one named last changes fastest.
Arguments:
- tokens: bfloat16 [12, 8192], P('group', 'gx'), parts along dimension 0, may hold values from -40 to 40
- norm_gain: float32 [8192], P('gx'), may hold values from 0.1 to 1.9
- q_weight: bfloat16 [8192, 4096], P('gx', ('gy', 'gz')), may hold values from -0.0625 to 0.0625
- kv_weight: bfloat16 [8192, 512], P('gx'), may hold values from -0.0625 to 0.0625
- out_weight: bfloat16 [4096, 8192], P(('gy', 'gz'), 'gx'), may hold values from -0.09375 to 0.09375
- gate_weight: bfloat16 [8192, 16384], P('gx', ('gy', 'gz')), may hold values from -0.0625 to 0.0625
- up_weight: bfloat16 [8192, 16384], P('gx', ('gy', 'gz')), may hold values from -0.0625 to 0.0625
- down_weight: bfloat16 [16384, 8192], P(('gy', 'gz'), 'gx'), may hold values from -0.046875 to 0.046875
- kv_cache: bfloat16 [12, 2048, 512], P(('group', 'gy'), ('gx', 'gz')), parts along dimension 0, may hold values from -55 to 55
- lengths: int32 [12], P(('group', 'gy')), parts along dimension 0, may hold values from 1026 to 2048, as said below
Outputs:
- mixed: bfloat16 [12, 8192], P('group', 'gx'), parts along dimension 0
- new_kv: bfloat16 [12, 512], P(('group', 'gy')), parts along dimension 0
There are 2 independent parts, one for each index of `group`. A program takes and returns all parts, laid end to end along the dimension named above; an argument that names none is the same for every part. Nothing has to cross between parts.
Inputs may be any that keep to these rules, and one draw needn't show every extreme that they name: The new token of sequence s stands at position lengths[s]; cache positions from lengths[s] on hold no valid token; some sequence has all 2048 positions valid.
All inputs are finite; a program needn't handle non-finite values.
Results may differ from a plain program's by a relative error of at most 0.012.
Values may be sent and summed in bfloat16 or wider, within the bound.
A program may use at most 128 MiB of HBM per device.

v0:
```python
import jax
import jax.numpy as jnp
from jax import lax
from jax.sharding import PartitionSpec as P

D = 8192
HEADS = 16
HEAD_DIM = 256


epsilon = 1e-05
masked_fill = -1e30
rotary_base = 10000.0


def joined(part, axis, combine):
    gathered = jax.tree.map(lambda a: lax.all_gather(a, axis), part)

    def take(source):
        return jax.tree.map(lambda a: lax.dynamic_index_in_dim(a, source, 0, False), gathered)

    return lax.fori_loop(
        1, lax.axis_size(axis), lambda source, state: combine(state, take(source)), take(0)
    )


def rotate(values, angle):
    middle = values.shape[-1] // 2
    first = values[..., :middle]
    second = values[..., middle:]
    cosine = jnp.cos(angle)
    sine_part = jnp.sin(angle)
    return jnp.concatenate(
        [first * cosine - second * sine_part, first * sine_part + second * cosine], -1
    )


def angles(lengths, head_dim):
    middle = head_dim // 2
    spread = rotary_base ** (-jnp.arange(middle, dtype=jnp.float32) / middle)
    return lengths.astype(jnp.float32)[:, None] * spread[None, :]


def combine(earlier, later):
    top = jnp.maximum(earlier[0], later[0])
    first_scale = jnp.exp(earlier[0] - top)
    second_scale = jnp.exp(later[0] - top)
    numer = earlier[1] * first_scale[..., None] + later[1] * second_scale[..., None]
    denom = earlier[2] * first_scale + later[2] * second_scale
    return (top, numer, denom)


def body(
    tokens,
    norm_gain,
    q_weight,
    kv_weight,
    out_weight,
    gate_weight,
    up_weight,
    down_weight,
    kv_cache,
    lengths,
):
    inputs = tokens.astype(jnp.float32)
    totals = lax.psum((jnp.sum(inputs, 1), jnp.sum(inputs * inputs, 1)), "gx")
    center = totals[0] / D
    spread_sq = totals[1] / D - center * center
    normed = (
        (inputs - center[:, None]) * lax.rsqrt(spread_sq + epsilon)[:, None] * norm_gain[None, :]
    ).astype(jnp.bfloat16)
    query_part = jnp.dot(normed, q_weight, preferred_element_type=jnp.float32)
    keyval_part = jnp.dot(normed, kv_weight, preferred_element_type=jnp.float32)
    gate_part = jnp.dot(normed, gate_weight, preferred_element_type=jnp.float32)
    up_part = jnp.dot(normed, up_weight, preferred_element_type=jnp.float32)
    query, keyval, gate, upward = lax.psum((query_part, keyval_part, gate_part, up_part), "gx")
    hidden = (jax.nn.silu(gate) * upward).astype(jnp.bfloat16)
    seq_dev = lengths.shape[0]
    row_groups = lax.axis_size("gy")
    block = q_weight.shape[1]
    first_row = lax.axis_index("gy") * seq_dev
    angle = angles(lengths, HEAD_DIM)
    own_keyval = lax.dynamic_slice_in_dim(keyval, first_row, seq_dev, 0)
    new_kv = jnp.concatenate(
        [rotate(own_keyval[:, :HEAD_DIM], angle), own_keyval[:, HEAD_DIM:]], 1
    ).astype(jnp.bfloat16)
    query_bf = query.astype(jnp.bfloat16)
    every_head = lax.all_gather(query_bf, ("gy", "gz"), axis=1, tiled=True)
    own_query = lax.dynamic_slice_in_dim(every_head, first_row, seq_dev, 0)
    rotated = rotate(
        own_query.astype(jnp.float32).reshape(seq_dev, HEADS, HEAD_DIM), angle[:, None, :]
    ).astype(jnp.bfloat16)
    ctx_dev = kv_cache.shape[1]
    offset = lax.axis_index(("gx", "gz")) * ctx_dev
    positions = offset + jnp.arange(ctx_dev, dtype=jnp.int32)
    live = positions[None, :] < lengths[:, None]
    scale = HEAD_DIM ** (-0.5)
    scores = (
        jnp.einsum(
            "shd,scd->shc", rotated, kv_cache[:, :, :HEAD_DIM], preferred_element_type=jnp.float32
        )
        * scale
    )
    key_new = new_kv[:, :HEAD_DIM]
    value_new = new_kv[:, HEAD_DIM:]
    own_score = (
        jnp.einsum("shd,sd->sh", rotated, key_new, preferred_element_type=jnp.float32) * scale
    )
    hidden_scores = jnp.where(live[:, None, :], scores, masked_fill)
    local_top = jnp.maximum(jnp.max(hidden_scores, 2), own_score)
    weights = jnp.where(live[:, None, :], jnp.exp(hidden_scores - local_top[..., None]), 0.0)
    numer = jnp.einsum(
        "shc,scd->shd",
        weights.astype(jnp.bfloat16),
        kv_cache[:, :, HEAD_DIM:],
        preferred_element_type=jnp.float32,
    )
    denom = jnp.sum(weights, 2)
    top, numer, denom = joined((local_top, numer, denom), ("gx", "gz"), combine)
    own_weight = jnp.exp(own_score - top)
    numer = numer + own_weight[..., None] * value_new.astype(jnp.float32)[:, None, :]
    denom = denom + own_weight
    attended = (numer / denom[..., None]).astype(jnp.bfloat16)
    grouped = attended.reshape(seq_dev, row_groups, HEADS * HEAD_DIM // row_groups)
    picked = lax.dynamic_slice_in_dim(grouped, lax.axis_index("gz") * block, block, 2)
    head_block = lax.all_to_all(picked, "gy", split_axis=1, concat_axis=0, tiled=True).reshape(
        seq_dev * row_groups, block
    )
    partial_value = jnp.dot(head_block, out_weight, preferred_element_type=jnp.float32) + jnp.dot(
        hidden, down_weight, preferred_element_type=jnp.float32
    )
    total = lax.psum(partial_value, ("gy", "gz"))
    mixed = (inputs + total).astype(jnp.bfloat16)
    return (mixed, new_kv)


def solution(mesh):
    in_specs = (
        P("group", "gx"),
        P("gx"),
        P("gx", ("gy", "gz")),
        P("gx", None),
        P(("gy", "gz"), "gx"),
        P("gx", ("gy", "gz")),
        P("gx", ("gy", "gz")),
        P(("gy", "gz"), "gx"),
        P(("group", "gy"), ("gx", "gz"), None),
        P(("group", "gy")),
    )
    out_specs = (P("group", "gx"), P(("group", "gy"), None))
    return jax.shard_map(body, mesh=mesh, in_specs=in_specs, out_specs=out_specs, check_vma=False)
```

profile of v0, /device:TPU:0, one launch (start us, length us, event | category | flops | bytes accessed | tf_op | source)
XLA Modules:
  0.0 137.5 jit_solution(9791205990848251122)
XLA Ops:
  7.2 1.1 convert_reduce_fusion
  8.3 13.5 %all-reduce.1 = (f32[6]{0:T(128)S(1)}, f32[6]{0:T(128)S(1)}) all-reduce(f32[6]{0:T(128)S(1)} %get-tuple-element.184, f32[6]{0:T(128)S(1)} %get-tuple-element.183), channel_id=1, replica_groups=mesh['group'=2,'gx'=4,'gy'=2,'gz'=2] {'gx'}, use_global_device_ids=true, to_apply=%region_3.0 | all-reduce | flops 12 | bytes 96 | tf_op jit(solution)/shard_map/psum | solution.py:66
  21.8 8.9 %fusion.29 = f32[6,4096]{1,0:T(8,128)} fusion(bf16[2048,4096]{1,0:T(8,128)(2,1)} %param.17, bf16[6,2048]{1,0:T(8,128)(2,1)} %param.12, f32[2048]{0:T(1024)} %param.13, f32[6]{0:T(128)S(1)} %get-tuple-element.220, f32[6]{0:T(128)S(1)} %get-tuple-element.219), kind=kOutput, calls=%fused_computation.63 | convolution fusion | flops 100724736 | bytes 16908336 | tf_op jit(solution)/shard_map/dot_general | solution.py:74
  30.7 1.7 %copy-done.1 = bf16[2048,4096]{1,0:T(8,128)(2,1)S(1)} copy-done((bf16[2048,4096]{1,0:T(8,128)(2,1)S(1)}, bf16[2048,4096]{1,0:T(8,128)(2,1)}, u32[]{:S(2)}) %copy-start.1) | copy-done | bytes 16777240
  32.4 3.0 %fusion.27 = f32[6,4096]{1,0:T(8,128)} fusion(bf16[2048,4096]{1,0:T(8,128)(2,1)S(1)} %copy-done.1, bf16[6,2048]{1,0:T(8,128)(2,1)S(1)} %copy-done.3, f32[2048]{0:T(1024)S(1)} %copy-done.4, f32[6]{0:T(128)S(1)} %get-tuple-element.220, f32[6]{0:T(128)S(1)} %get-tuple-element.219), kind=kOutput, calls=%fused_computation.62 | convolution fusion | flops 100724736 | bytes 16908336 | tf_op jit(solution)/shard_map/dot_general | solution.py:75
  35.4 2.9 %fusion.33 = f32[6,1024]{1,0:T(8,128)S(1)} fusion(bf16[2048,1024]{1,0:T(8,128)(2,1)} %param.14, bf16[6,2048]{1,0:T(8,128)(2,1)S(1)} %copy-done.3, f32[2048]{0:T(1024)S(1)} %copy-done.4, f32[6]{0:T(128)S(1)} %get-tuple-element.220, f32[6]{0:T(128)S(1)} %get-tuple-element.219), kind=kOutput, calls=%fused_computation.65 | convolution fusion | flops 25227264 | bytes 4251696 | tf_op jit(solution)/shard_map/dot_general | solution.py:72
  38.3 0.4 fusion.31
  38.7 16.4 %all-reduce = (bf16[6,1024]{1,0:T(8,128)(2,1)S(1)}, f32[6,512]{1,0:T(8,128)S(1)}) all-reduce(f32[6,1024]{1,0:T(8,128)S(1)} %fusion.33, f32[6,512]{1,0:T(8,128)S(1)} %fusion.31), channel_id=1, replica_groups=mesh['group'=2,'gx'=4,'gy'=2,'gz'=2] {'gx'}, use_global_device_ids=true, to_apply=%region_4.0 | all-reduce | flops 9216 | bytes 61440 | tf_op jit(solution)/shard_map/psum | solution.py:76
  55.1 5.2 %all_gather.21 = bf16[6,4096]{1,0:T(8,128)(2,1)S(1)} all-gather(bf16[6,1024]{1,0:T(8,128)(2,1)S(1)} %get-tuple-element.199), channel_id=1, replica_groups=mesh['group'=2,'gx'=4,'gy'=2,'gz'=2] {'gy','gz'}, dimensions={1}, use_global_device_ids=true | all-gather | bytes 61440 | tf_op jit(solution)/shard_map/all_gather | solution.py:88
  60.7 0.3 fusion.38
  61.0 0.2 fusion.14
  61.2 0.2 fusion.4
  61.5 12.8 %all-gather.4 = f32[8,3,16]{2,1,0:T(4,128)S(1)} all-gather(f32[1,3,16]{2,1,0:T(4,128)S(1)} %bitcast.56), channel_id=4, replica_groups=mesh['group'=2,'gx'=4,'gy'=2,'gz'=2] {'gx','gz'}, dimensions={0}, use_global_device_ids=true | all-gather | bytes 1728 | tf_op jit(solution)/shard_map/all_gather | solution.py:17
  74.2 14.4 %all-gather.1 = f32[24,16,256]{2,1,0:T(8,128)S(1)} all-gather(f32[3,16,256]{2,1,0:T(8,128)S(1)} %fusion.4), channel_id=3, replica_groups=mesh['group'=2,'gx'=4,'gy'=2,'gz'=2] {'gx','gz'}, dimensions={0}, use_global_device_ids=true | all-gather | bytes 442368 | tf_op jit(solution)/shard_map/all_gather | solution.py:17
  88.7 12.8 %all-gather.3 = f32[8,3,16]{2,1,0:T(4,128)S(1)} all-gather(f32[1,3,16]{2,1,0:T(4,128)S(1)} %bitcast.55), channel_id=2, replica_groups=mesh['group'=2,'gx'=4,'gy'=2,'gz'=2] {'gx','gz'}, dimensions={0}, use_global_device_ids=true | all-gather | bytes 1728 | tf_op jit(solution)/shard_map/all_gather | solution.py:17
  101.4 0.9 while.19
  102.6 0.6 copy.16
  103.2 3.2 %all-to-all-start = ((bf16[3,2,1024]{2,0,1:T(4,128)(2,1)}), bf16[3,2,1024]{2,0,1:T(4,128)(2,1)S(1)}, u32[]{:S(2)}, u32[]{:S(2)}) async-start(bf16[3,2,1024]{2,0,1:T(4,128)(2,1)} %copy.16), calls=%async_computation | async-start | bytes 32768 | tf_op jit(solution)/shard_map/all_to_all | solution.py:126
  106.5 0.6 pad_maximum_fusion.3
  107.1 3.2 %all-to-all-done = bf16[3,2,1024]{2,0,1:T(4,128)(2,1)S(1)} async-done(((bf16[3,2,1024]{2,0,1:T(4,128)(2,1)}), bf16[3,2,1024]{2,0,1:T(4,128)(2,1)S(1)}, u32[]{:S(2)}, u32[]{:S(2)}) %all-to-all-start) | async-done | bytes 12320 | tf_op jit(solution)/shard_map/all_to_all | solution.py:126
  110.4 8.3 %fusion.12 = f32[6,2048]{1,0:T(8,128)S(1)} fusion(bf16[4096,2048]{1,0:T(8,128)(2,1)} %param.19, f32[6,4096]{1,0:T(8,128)} %get-tuple-element.203, f32[6,4096]{1,0:T(8,128)} %get-tuple-element.204), kind=kOutput, calls=%fused_computation.24 | convolution fusion | flops 100810752 | bytes 17022976 | tf_op jit(solution)/shard_map/dot_general | solution.py:129
  118.7 0.7 convolution_add_fusion
  119.4 10.7 %psum.55 = f32[6,2048]{1,0:T(8,128)S(1)} all-reduce(f32[6,2048]{1,0:T(8,128)S(1)} %convolution_add_fusion), channel_id=1, replica_groups=mesh['group'=2,'gx'=4,'gy'=2,'gz'=2] {'gy','gz'}, use_global_device_ids=true, to_apply=%region_12.13 | all-reduce | flops 12288 | bytes 98304 | tf_op jit(solution)/shard_map/psum | solution.py:132
  130.1 0.6 fusion.11
  (51 shorter events, 1.5 us)
Async XLA Ops:
  7.2 31.1 %copy-start = (bf16[2048,512]{1,0:T(8,128)(2,1)S(1)}, bf16[2048,512]{1,0:T(8,128)(2,1)}, u32[]{:S(2)}) copy-start(bf16[2048,512]{1,0:T(8,128)(2,1)} %param.15) | copy-start | bytes 6291460
  7.2 23.5 %copy-start.3 = (bf16[6,2048]{1,0:T(8,128)(2,1)S(1)}, bf16[6,2048]{1,0:T(8,128)(2,1)}, u32[]{:S(2)}) copy-start(bf16[6,2048]{1,0:T(8,128)(2,1)} %param.12) | copy-start | bytes 73732
  7.2 23.5 %copy-start.4 = (f32[2048]{0:T(1024)S(1)}, f32[2048]{0:T(1024)}, u32[]{:S(2)}) copy-start(f32[2048]{0:T(1024)} %param.13) | copy-start | bytes 24580
  7.2 103.2 %all-reduce.5.cloned.1.call-start = ((), (), s32[]{:S(2)}) async-start(), calls=%async_computation.1 | async-start | bytes 524288 | tf_op jit(solution)/shard_map/psum | solution.py:76
  21.8 10.6 %copy-start.1 = (bf16[2048,4096]{1,0:T(8,128)(2,1)S(1)}, bf16[2048,4096]{1,0:T(8,128)(2,1)}, u32[]{:S(2)}) copy-start(bf16[2048,4096]{1,0:T(8,128)(2,1)} %param.18) | copy-start | bytes 50331652
  32.4 6.3 %copy-start.6 = (s32[3]{0:T(128)S(1)}, s32[3]{0:T(128)}, u32[]{:S(2)}) copy-start(s32[3]{0:T(128)} %param.21) | copy-start | bytes 40
  32.4 28.3 %copy-start.5 = (bf16[3,256,512]{2,1,0:T(8,128)(2,1)S(1)}, bf16[3,256,512]{2,1,0:T(8,128)(2,1)}, u32[]{:S(2)}) copy-start(bf16[3,256,512]{2,1,0:T(8,128)(2,1)} %param.20) | copy-start | bytes 2359300
  103.2 7.1 %all-to-all-start = ((bf16[3,2,1024]{2,0,1:T(4,128)(2,1)}), bf16[3,2,1024]{2,0,1:T(4,128)(2,1)S(1)}, u32[]{:S(2)}, u32[]{:S(2)}) async-start(bf16[3,2,1024]{2,0,1:T(4,128)(2,1)} %copy.16), calls=%async_computation | async-start | bytes 32768 | tf_op jit(solution)/shard_map/all_to_all | solution.py:126
  110.4 8.3 %copy-start.2 = (bf16[1024,2048]{1,0:T(8,128)(2,1)S(1)}, bf16[1024,2048]{1,0:T(8,128)(2,1)}, u32[]{:S(2)}) copy-start(bf16[1024,2048]{1,0:T(8,128)(2,1)} %param.16) | copy-start | bytes 12582916
Sparse Core Ops, SparseCore 0:
  35.5 34.4 all-reduce.4
where the time goes:
time: 138 us
  blocking collectives  85.7 us (62%)
  matrix products  24.8 us (18%)
  between operations  14.2 us (10%)
  other arithmetic  3.69 us (3%)
  waiting for transfers between devices  3.28 us (2%)
  starting transfers between devices  3.27 us (2%)
  local copies, waits for them, and re-layouts  2.41 us (2%)
    all_gather x3, blocking collectives, joined(): gathered = jax.tree.map(lambda a: lax.all_gather(a, axis), part)  40 us
    psum x1, blocking collectives, body(): lax.psum((query_part, keyval_part, gate_part, up_part), 'gx')  16.4 us
    psum x1, blocking collectives, body(): totals = lax.psum((jnp.sum(inputs, 1), jnp.sum(inputs * inputs, 1)), 'gx')  13.5 us
    psum x1, blocking collectives, body(): total = lax.psum(partial_value, ('gy', 'gz'))  10.7 us
    dot_general x1, matrix products, body(): gate_part = jnp.dot(normed, gate_weight, preferred_element_type=jnp.float32)  8.91 us
    dot_general x1, matrix products, body(): jnp.dot(hidden, down_weight, preferred_element_type=jnp.float32)  8.31 us
    all_gather x1, blocking collectives, body(): every_head = lax.all_gather(query_bf, ('gy', 'gz'), axis=1, tiled=True)  5.24 us
    all_to_all x1, waiting for transfers between devices, body(): lax.all_to_all(picked, 'gy', split_axis=1, concat_axis=0, tiled=True)  3.24 us
  transfers between devices with their start and end apart: 2, of which 1 were waited for; matrix products, arithmetic and copies ran while one was open for 5% of the time, Pallas kernels for 0%

commit v1 on v0

--- a/solution.py
+++ b/solution.py
@@ -1,6 +1,11 @@
+import functools
+import itertools
+
 import jax
 import jax.numpy as jnp
 from jax import lax
+from jax.experimental import pallas as pl
+from jax.experimental.pallas import tpu as pltpu
 from jax.sharding import PartitionSpec as P
 
 D = 8192
@@ -134,7 +139,555 @@
     return (mixed, new_kv)
 
 
+MESH = pl.DeviceIdType.MESH
+F32 = jnp.float32
+BF16 = jnp.bfloat16
+
+
+def kernel(
+    dims,
+    lengths_ref,
+    tokens_h,
+    gain_h,
+    spread_h,
+    q_h,
+    kv_h,
+    cache_h,
+    gate_h,
+    up_h,
+    out_h,
+    down_h,
+    mixed_ref,
+    newkv_ref,
+    tokens_v,
+    gain_v,
+    spread_v,
+    q_v,
+    kv_v,
+    cache_v,
+    gate_v,
+    up_v,
+    out_v,
+    down_v,
+    load_sem,
+    gu_sem,
+    down_sem,
+    x_v,
+    normed_v,
+    stat_v,
+    qp_v,
+    qrs_v,
+    kvs_v,
+    qsend_v,
+    qall_v,
+    rot_v,
+    newkv_v,
+    part_v,
+    prs_v,
+    att_v,
+    attall_v,
+    gsend_v,
+    grs_v,
+    own_v,
+    hid_v,
+    acc_v,
+    fin_v,
+    stat_sem,
+    q_sem,
+    kvx_sem,
+    qa_sem,
+    p_sem,
+    a_sem,
+    a_recv,
+    g_sem,
+    h_sem,
+    f_sem,
+):
+    ngx, ngy, ngz, rows, rp = dims
+    gx, gy, gz = lax.axis_index("gx"), lax.axis_index("gy"), lax.axis_index("gz")
+    dx = x_v.shape[1]
+    qd = q_v.shape[1]
+    heads_dev = qd // HEAD_DIM
+    own_heads = heads_dev // ngx
+    seq_dev = cache_v.shape[0]
+    ctx_dev = cache_v.shape[1]
+    fb = gate_v.shape[2]
+    owners = ngx * ngz
+    part_heads = HEADS // owners
+    first = gy * seq_dev
+    scale = HEAD_DIM ** (-0.5)
+    middle = HEAD_DIM // 2
+
+    small = [
+        pltpu.make_async_copy(a, b, load_sem.at[i])
+        for i, (a, b) in enumerate(
+            (
+                (tokens_h, tokens_v),
+                (gain_h, gain_v),
+                (spread_h, spread_v),
+                (q_h, q_v),
+                (kv_h, kv_v),
+                (cache_h, cache_v),
+                (out_h, out_v),
+            )
+        )
+    ]
+
+    def gu_copies(step):
+        block = lax.rem(gx + 1 + step, ngx)
+        columns = pl.ds(pl.multiple_of(block * fb, fb), fb)
+        return (
+            pltpu.make_async_copy(gate_h.at[:, columns], gate_v.at[step], gu_sem.at[0, step]),
+            pltpu.make_async_copy(up_h.at[:, columns], up_v.at[step], gu_sem.at[1, step]),
+        )
+
+    def down_copy(step):
+        block = lax.rem(gx + step, ngx)
+        picked = pl.ds(pl.multiple_of(block * fb, fb), fb)
+        return pltpu.make_async_copy(down_h.at[picked], down_v.at[step], down_sem.at[step])
+
+    for copy in small[:6]:
+        copy.start()
+    for step in range(ngx):
+        for copy in gu_copies(step):
+            copy.start()
+    small[6].start()
+    for step in range(ngx):
+        down_copy(step).start()
+
+    offsets = [o for o in itertools.product(range(ngx), range(ngy), range(ngz)) if any(o)]
+
+    def shifted(ox, oy, oz):
+        return lax.rem(gx + ox, ngx), lax.rem(gy + oy, ngy), lax.rem(gz + oz, ngz)
+
+    def at(px, py, pz):
+        return {"gx": px, "gy": py, "gz": pz}
+
+    barrier = pltpu.get_barrier_semaphore()
+    for offset in offsets:
+        pl.semaphore_signal(barrier, inc=1, device_id=at(*shifted(*offset)), device_id_type=MESH)
+
+    small[0].wait()
+    x_v[...] = jnp.zeros_like(x_v)
+    x_v[0:rows, :] = tokens_v[...].astype(F32)
+    x = x_v[...]
+    lane = lax.broadcasted_iota(jnp.int32, (rp, 128), 1)
+    stat_v[gx] = jnp.where(
+        lane < 64, jnp.sum(x, 1, keepdims=True), jnp.sum(x * x, 1, keepdims=True)
+    )
+    pl.semaphore_wait(barrier, len(offsets))
+
+    pending = []
+
+    def send(source, target, sends, receives, device):
+        copy = pltpu.make_async_remote_copy(
+            src_ref=source,
+            dst_ref=target,
+            send_sem=sends,
+            recv_sem=receives,
+            device_id=device,
+            device_id_type=MESH,
+        )
+        copy.start()
+        pending.append(copy)
+
+    def arrived(slot, receives):
+        pltpu.make_async_remote_copy(
+            src_ref=slot,
+            dst_ref=slot,
+            send_sem=receives,
+            recv_sem=receives,
+            device_id=at(gx, gy, gz),
+            device_id_type=MESH,
+        ).wait_recv()
+
+    for k in range(1, ngx):
+        peer = lax.rem(gx + k, ngx)
+        send(stat_v.at[gx], stat_v.at[gx], stat_sem.at[0, peer], stat_sem.at[1, gx], at(peer, gy, gz))
+    small[1].wait()
+    small[2].wait()
+
+    row = lax.broadcasted_iota(jnp.int32, (rp, middle), 0)
+    length = jnp.zeros((rp, middle), jnp.int32)
+    for s in range(seq_dev):
+        length = jnp.where(row == first + s, lengths_ref[s], length)
+    angle = length.astype(F32) * spread_v[...]
+    cosine = jnp.cos(angle)
+    sine = jnp.sin(angle)
+
+    for k in range(1, ngx):
+        peer = lax.rem(gx + k, ngx)
+        arrived(stat_v.at[peer], stat_sem.at[1, peer])
+    totals = stat_v[0]
+    for k in range(1, ngx):
+        totals = totals + stat_v[k]
+    center = totals[:, 0:1] / D
+    spread_sq = totals[:, 64:65] / D - center * center
+    normed_v[...] = ((x_v[...] - center) * lax.rsqrt(spread_sq + epsilon) * gain_v[...]).astype(BF16)
+
+    qo = own_heads * HEAD_DIM
+    small[3].wait()
+
+    @pl.loop(0, ngx)
+    def _(j):
+        columns = pl.ds(pl.multiple_of(j * qo, qo), qo)
+        qp_v[j] = jnp.dot(normed_v[...], q_v[:, columns], preferred_element_type=F32)
+
+    for k in range(1, ngx):
+        peer = lax.rem(gx + k, ngx)
+        send(qp_v.at[peer], qrs_v.at[gx], q_sem.at[0, peer], q_sem.at[1, gx], at(peer, gy, gz))
+    small[4].wait()
+    kvs_v[gx] = jnp.dot(normed_v[...], kv_v[...], preferred_element_type=F32)
+    for k in range(1, ngx):
+        peer = lax.rem(gx + k, ngx)
+        send(kvs_v.at[gx], kvs_v.at[gx], kvx_sem.at[0, peer], kvx_sem.at[1, gx], at(peer, gy, gz))
+
+    tile = min(512, fb)
+
+    def gate_up(step):
+        for copy in gu_copies(step):
+            copy.wait()
+
+        @pl.loop(0, fb // tile)
+        def _(n):
+            columns = pl.ds(pl.multiple_of(n * tile, tile), tile)
+            g = jnp.dot(normed_v[...], gate_v[step, :, columns], preferred_element_type=F32)
+            u = jnp.dot(normed_v[...], up_v[step, :, columns], preferred_element_type=F32)
+            both = jnp.concatenate([g, u], 0)
+            if step < ngx - 1:
+                gsend_v[step, :, columns] = both.astype(BF16)
+            else:
+                own_v[:, columns] = both
+
+        if step < ngx - 1:
+            peer = lax.rem(gx + 1 + step, ngx)
+            send(gsend_v.at[step], grs_v.at[gx], g_sem.at[0, peer], g_sem.at[1, gx], at(peer, gy, gz))
+
+    def gather_query():
+        total = qp_v[gx]
+        for k in range(1, ngx):
+            peer = lax.rem(gx + k, ngx)
+            arrived(qrs_v.at[peer], q_sem.at[1, peer])
+            total = total + qrs_v[peer]
+        mine = (gy * ngz + gz) * heads_dev + gx * own_heads
+        for h in range(own_heads):
+            piece = total[:, h * HEAD_DIM : (h + 1) * HEAD_DIM].astype(BF16)
+            qsend_v[h] = piece
+            qall_v[mine + h] = piece
+        for offset in offsets:
+            px, py, pz = shifted(*offset)
+            send(
+                qsend_v,
+                qall_v.at[pl.ds(mine, own_heads)],
+                qa_sem.at[0, px, py, pz],
+                qa_sem.at[1, gx, gy, gz],
+                at(px, py, pz),
+            )
+
+    me_owner = gx * ngz + gz
+
+    def attend():
+        keyval = kvs_v[gx]
+        for k in range(1, ngx):
+            peer = lax.rem(gx + k, ngx)
+            arrived(kvs_v.at[peer], kvx_sem.at[1, peer])
+            keyval = keyval + kvs_v[peer]
+        a = keyval[:, :middle]
+        b = keyval[:, middle:HEAD_DIM]
+        newkv_v[:, :middle] = a * cosine - b * sine
+        newkv_v[:, middle:HEAD_DIM] = a * sine + b * cosine
+        newkv_v[:, HEAD_DIM:] = keyval[:, HEAD_DIM:]
+        picked = newkv_v[0:seq_dev, :]
+        for y in range(1, ngy):
+            picked = jnp.where(gy == y, newkv_v[y * seq_dev : (y + 1) * seq_dev, :], picked)
+        newkv_ref[...] = picked.astype(BF16)
+        for offset in offsets:
+            px, py, pz = shifted(*offset)
+            slot = (py * ngz + pz) * heads_dev + px * own_heads
+            arrived(qall_v.at[pl.ds(slot, own_heads)], qa_sem.at[1, px, py, pz])
+        q3 = qall_v[...].astype(F32)
+        a = q3[:, :, :middle]
+        b = q3[:, :, middle:]
+        rot_v[:, :, :middle] = (a * cosine - b * sine).astype(BF16).astype(F32)
+        rot_v[:, :, middle:] = (a * sine + b * cosine).astype(BF16).astype(F32)
+        small[5].wait()
+        rotated = rot_v[...].reshape(HEADS * rp, HEAD_DIM).astype(BF16)
+        rowid = lax.rem(lax.broadcasted_iota(jnp.int32, (HEADS * rp, ctx_dev), 0), rp)
+        position = (gx * ngz + gz) * ctx_dev + lax.broadcasted_iota(
+            jnp.int32, (HEADS * rp, ctx_dev), 1
+        )
+        scores = jnp.full((HEADS * rp, ctx_dev), masked_fill, F32)
+        limit = jnp.zeros((HEADS * rp, ctx_dev), jnp.int32)
+        for s in range(seq_dev):
+            raw = lax.dot_general(
+                rotated,
+                cache_v[s, :, :HEAD_DIM],
+                (((1,), (1,)), ((), ())),
+                preferred_element_type=F32,
+            )
+            limit = jnp.where(rowid == first + s, lengths_ref[s], limit)
+            scores = jnp.where(rowid == first + s, raw * scale, scores)
+        live = position < limit
+        scores = jnp.where(live, scores, masked_fill)
+        top = jnp.max(scores, 1, keepdims=True)
+        weights = jnp.where(live, jnp.exp(scores - top), 0.0)
+        denom = jnp.sum(weights, 1, keepdims=True)
+        numer = jnp.zeros((HEADS * rp, HEAD_DIM), F32)
+        for s in range(seq_dev):
+            numer = numer + jnp.dot(
+                jnp.where(rowid == first + s, weights, 0.0).astype(BF16),
+                cache_v[s, :, HEAD_DIM:],
+                preferred_element_type=F32,
+            )
+        lanes = lax.broadcasted_iota(jnp.int32, (HEADS * rp, 128), 1)
+        part_v[:, :, :HEAD_DIM] = numer.reshape(HEADS, rp, HEAD_DIM)
+        part_v[:, :, HEAD_DIM:] = jnp.where(lanes < 64, top, denom).reshape(HEADS, rp, 128)
+        for ox, oz in itertools.product(range(ngx), range(ngz)):
+            if ox or oz:
+                px, py, pz = shifted(ox, 0, oz)
+                peer = px * ngz + pz
+                send(
+                    part_v.at[pl.ds(peer * part_heads, part_heads)],
+                    prs_v.at[me_owner],
+                    p_sem.at[0, peer],
+                    p_sem.at[1, me_owner],
+                    at(px, py, pz),
+                )
+
+    block = (me_owner * part_heads) // heads_dev
+    by, bz = block // ngz, lax.rem(block, ngz)
+    local = lax.rem(me_owner, heads_dev // part_heads)
+
+    def combine_parts():
+        prs_v[me_owner] = part_v[pl.ds(me_owner * part_heads, part_heads)]
+        for ox, oz in itertools.product(range(ngx), range(ngz)):
+            if ox or oz:
+                px, py, pz = shifted(ox, 0, oz)
+                peer = px * ngz + pz
+                arrived(prs_v.at[peer], p_sem.at[1, peer])
+        rot = rot_v[pl.ds(me_owner * part_heads, part_heads)]
+        newkv = newkv_v[...].astype(BF16).astype(F32)
+        own = jnp.sum(rot * newkv[:, :HEAD_DIM], 2, keepdims=True) * scale
+        tops = [prs_v[o, :, :, HEAD_DIM : HEAD_DIM + 1] for o in range(owners)]
+        top = own
+        for t in tops:
+            top = jnp.maximum(top, t)
+        weight = jnp.exp(own - top)
+        numer = weight * newkv[:, HEAD_DIM:]
+        denom = weight
+        for o in range(owners):
+            factor = jnp.exp(tops[o] - top)
+            numer = numer + factor * prs_v[o, :, :, :HEAD_DIM]
+            denom = denom + factor * prs_v[o, :, :, HEAD_DIM + 64 : HEAD_DIM + 65]
+        rowid = lax.broadcasted_iota(jnp.int32, (part_heads, rp, HEAD_DIM), 1)
+        mine = (rowid >= first) & (rowid < first + seq_dev)
+        att_v[...] = jnp.where(mine, numer / denom, 0.0).astype(BF16)
+        for k in range(ngx):
+            px = lax.rem(gx + k, ngx)
+            copy = pltpu.make_async_remote_copy(
+                src_ref=att_v,
+                dst_ref=attall_v.at[gy, local],
+                send_sem=a_sem.at[px],
+                recv_sem=a_recv.at[gy, local],
+                device_id=at(px, by, bz),
+                device_id_type=MESH,
+            )
+            if k:
+                copy.start()
+                pending.append(copy)
+            else:
+                same = (by == gy) & (bz == gz)
+
+                @pl.when(same)
+                def _():
+                    attall_v[gy, local] = att_v[...]
+
+                @pl.when(jnp.logical_not(same))
+                def _(copy=copy):
+                    copy.start()
+                    copy.wait_send()
+
+    def out_product():
+        for sy in range(ngy):
+            for sl in range(heads_dev // part_heads):
+                owner = (gy * ngz + gz) * (heads_dev // part_heads) + sl
+                theirs = (sy == gy) & (owner == me_owner)
+
+                @pl.when(jnp.logical_not(theirs))
+                def _(sy=sy, sl=sl):
+                    arrived(attall_v.at[sy, sl], a_recv.at[sy, sl])
+
+        pieces = []
+        for h in range(heads_dev):
+            total = attall_v[0, h // part_heads, h % part_heads].astype(F32)
+            for sy in range(1, ngy):
+                total = total + attall_v[sy, h // part_heads, h % part_heads].astype(F32)
+            pieces.append(total.astype(BF16))
+        mixed_heads = jnp.concatenate(pieces, 1)
+        small[6].wait()
+        ct = min(512, dx)
+        normed_v[:, :qd] = mixed_heads
+
+        @pl.loop(0, dx // ct)
+        def _(n):
+            columns = pl.ds(pl.multiple_of(n * ct, ct), ct)
+            acc_v[:, columns] = jnp.dot(
+                normed_v[:, :qd], out_v[:, columns], preferred_element_type=F32
+            )
+
+    gate_up(0)
+    gather_query()
+    gate_up(1)
+    attend()
+    gate_up(2)
+    combine_parts()
+    for step in range(3, ngx):
+        gate_up(step)
+
+    both = own_v[...]
+    for k in range(1, ngx):
+        peer = lax.rem(gx + k, ngx)
+        arrived(grs_v.at[peer], g_sem.at[1, peer])
+        both = both + grs_v[peer].astype(F32)
+    g = both[:rp]
+    u = both[rp:]
+    hid_v[gx] = (g / (1.0 + jnp.exp(-g)) * u).astype(BF16)
+    for k in range(1, ngx):
+        peer = lax.rem(gx + k, ngx)
+        send(hid_v.at[gx], hid_v.at[gx], h_sem.at[0, peer], h_sem.at[1, gx], at(peer, gy, gz))
+
+    out_product()
+    spot = gy * ngz + gz
+    ct = min(512, dx)
+    for step in range(ngx):
+        source = lax.rem(gx + step, ngx)
+        down_copy(step).wait()
+        if step:
+            arrived(hid_v.at[source], h_sem.at[1, source])
+
+        @pl.loop(0, dx // ct)
+        def _(n):
+            columns = pl.ds(pl.multiple_of(n * ct, ct), ct)
+            acc_v[:, columns] += jnp.dot(
+                hid_v[source], down_v[step, :, columns], preferred_element_type=F32
+            )
+
+    fin_v[spot] = acc_v[...].astype(BF16)
+    peers = [o for o in itertools.product(range(ngy), range(ngz)) if any(o)]
+    for oy, oz in peers:
+        px, py, pz = shifted(0, oy, oz)
+        peer = py * ngz + pz
+        send(fin_v.at[spot], fin_v.at[spot], f_sem.at[0, peer], f_sem.at[1, spot], at(px, py, pz))
+    total = x_v[...] + acc_v[...]
+    for oy, oz in peers:
+        px, py, pz = shifted(0, oy, oz)
+        peer = py * ngz + pz
+        arrived(fin_v.at[peer], f_sem.at[1, peer])
+        total = total + fin_v[peer].astype(F32)
+    mixed_ref[...] = total[:rows].astype(BF16)
+    for copy in pending:
+        copy.wait_send()
+
+
+def fused(sizes, *args):
+    (tokens, gain, qw, kvw, outw, gatew, upw, downw, cache, lengths) = args
+    ngx, ngy, ngz = sizes
+    rows, dx = tokens.shape
+    rp = -(-rows // 8) * 8
+    qd = qw.shape[1]
+    fb = gatew.shape[1] // ngx
+    own_heads = qd // HEAD_DIM // ngx
+    heads_dev = qd // HEAD_DIM
+    owners = ngx * ngz
+    part_heads = HEADS // owners
+    middle = HEAD_DIM // 2
+    spread = (rotary_base ** (-jnp.arange(middle, dtype=F32) / middle)).reshape(1, middle)
+    dma = pltpu.SemaphoreType.DMA
+    vm = pltpu.VMEM
+    scratch = [
+        vm(tokens.shape, BF16),
+        vm((1, dx), F32),
+        vm((1, middle), F32),
+        vm(qw.shape, BF16),
+        vm(kvw.shape, BF16),
+        vm(cache.shape, BF16),
+        vm((ngx, dx, fb), BF16),
+        vm((ngx, dx, fb), BF16),
+        vm(outw.shape, BF16),
+        vm((ngx, fb, dx), BF16),
+        dma((7,)),
+        dma((2, ngx)),
+        dma((ngx,)),
+        vm((rp, dx), F32),
+        vm((rp, dx), BF16),
+        vm((ngx, rp, 128), F32),
+        vm((ngx, rp, own_heads * HEAD_DIM), F32),
+        vm((ngx, rp, own_heads * HEAD_DIM), F32),
+        vm((ngx, rp, 2 * HEAD_DIM), F32),
+        vm((own_heads, rp, HEAD_DIM), BF16),
+        vm((HEADS, rp, HEAD_DIM), BF16),
+        vm((HEADS, rp, HEAD_DIM), F32),
+        vm((rp, 2 * HEAD_DIM), F32),
+        vm((HEADS, rp, HEAD_DIM + 128), F32),
+        vm((owners, part_heads, rp, HEAD_DIM + 128), F32),
+        vm((part_heads, rp, HEAD_DIM), BF16),
+        vm((ngy, heads_dev // part_heads, part_heads, rp, HEAD_DIM), BF16),
+        vm((ngx - 1, 2 * rp, fb), BF16),
+        vm((ngx, 2 * rp, fb), BF16),
+        vm((2 * rp, fb), F32),
+        vm((ngx, rp, fb), BF16),
+        vm((rp, dx), F32),
+        vm((ngy * ngz, rp, dx), BF16),
+        dma((2, ngx)),
+        dma((2, ngx)),
+        dma((2, ngx)),
+        dma((2, ngx, ngy, ngz)),
+        dma((2, owners)),
+        dma((ngx,)),
+        dma((ngy, heads_dev // part_heads)),
+        dma((2, ngx)),
+        dma((2, ngx)),
+        dma((2, ngy * ngz)),
+    ]
+    anywhere = pl.BlockSpec(memory_space=pl.ANY)
+    return pl.pallas_call(
+        functools.partial(kernel, (ngx, ngy, ngz, rows, rp)),
+        out_shape=(
+            jax.ShapeDtypeStruct(tokens.shape, BF16),
+            jax.ShapeDtypeStruct((cache.shape[0], 2 * HEAD_DIM), BF16),
+        ),
+        in_specs=[pl.BlockSpec(memory_space=pltpu.SMEM)] + [anywhere] * 10,
+        out_specs=(pl.BlockSpec(memory_space=pltpu.VMEM),) * 2,
+        scratch_shapes=scratch,
+        compiler_params=pltpu.CompilerParams(
+            collective_id=0, has_side_effects=True, vmem_limit_bytes=67043328
+        ),
+    )(lengths, tokens, gain.reshape(1, dx), spread, qw, kvw, cache, gatew, upw, outw, downw)
+
+
+def fits(sizes, q_dev, ff_dev, weight_bytes):
+    ngx, ngy, ngz = sizes
+    heads_dev = q_dev // HEAD_DIM
+    return (
+        ngx >= 3
+        and heads_dev % ngx == 0
+        and HEADS % (ngx * ngz) == 0
+        and heads_dev % (HEADS // (ngx * ngz)) == 0
+        and ff_dev % (ngx * 128) == 0
+        and weight_bytes <= 60 * 2**20
+    )
+
+
+def choose(sizes, *args):
+    held = sum(a.size * a.dtype.itemsize for a in args[2:9])
+    if fits(sizes, args[2].shape[1], args[5].shape[1], held):
+        return fused(sizes, *args)
+    return body(*args)
+
+
 def solution(mesh):
+    sizes = tuple(mesh.shape[a] for a in ("gx", "gy", "gz"))
+    chosen = functools.partial(choose, sizes)
     in_specs = (
         P("group", "gx"),
         P("gx"),
@@ -148,4 +701,4 @@
         P(("group", "gy")),
     )
     out_specs = (P("group", "gx"), P(("group", "gy"), None))
-    return jax.shard_map(body, mesh=mesh, in_specs=in_specs, out_specs=out_specs, check_vma=False)
+    return jax.shard_map(chosen, mesh=mesh, in_specs=in_specs, out_specs=out_specs, check_vma=False)

time: 138 us -> 47.5 us (0.34)
  blocking collectives: 85.7 us -> 0 us
  Pallas kernels: 0 us -> 43.5 us
  matrix products: 24.8 us -> 0 us
  between operations: 14.2 us -> 0.64 us
  waiting for transfers between devices: 3.28 us -> 0 us
  starting transfers between devices: 3.27 us -> 0 us
  other arithmetic: 3.69 us -> 0.53 us
    all_gather x4 -> x0, blocking collectives: 45.2 us -> none  [the longest x3 40 us: joined(): gathered = jax.tree.map(lambda a: lax.all_gather(a, axis), part)]
    pallas_call x0 -> x1, Pallas kernels: none -> 43.5 us  [fused(): pl.pallas_call(functools.partial(kernel, (ngx, ngy, ngz, rows, rp)), out_...]
    psum x3 -> x0, blocking collectives: 40.5 us -> none  [the longest x1 16.4 us: body(): lax.psum((query_part, keyval_part, gate_part, up_part), 'gx')]
    dot_general x9 -> x0, matrix products: 24.8 us -> none  [the longest x1 8.91 us: body(): gate_part = jnp.dot(normed, gate_weight, preferred_element_type=jnp.float32)]
    all_to_all x1 -> x0, waiting for transfers between devices: 3.24 us -> none  [body(): lax.all_to_all(picked, 'gy', split_axis=1, concat_axis=0, tiled=True)]
    all_to_all x1 -> x0, starting transfers between devices: 3.24 us -> none  [body(): lax.all_to_all(picked, 'gy', split_axis=1, concat_axis=0, tiled=True)]
  transfers between devices with their start and end apart: 2 -> 0, of which waited for: 1 -> 0; matrix products, arithmetic and copies ran while one was open for 5% -> 0% of each run, Pallas kernels for 0% -> 0%
where the time goes in v1:
time: 47.5 us; the launch traced here: 47.3 us
  Pallas kernels  43.5 us (92%)
  local copies, waits for them, and re-layouts  2.65 us (6%)
  between operations  0.64 us (1%)
  other arithmetic  0.53 us (1%)
    pallas_call x1, Pallas kernels, fused(): pl.pallas_call(functools.partial(kernel, (ngx, ngy, ngz, rows, rp)), out_...  43.5 us
    unnamed x2, local copies, waits for them, and re-layouts  2.65 us

profile of v1, /device:TPU:0, one launch (start us, length us, event | category | flops | bytes accessed | tf_op | source)
XLA Modules:
  0.0 47.3 jit_solution(12008488054673985698)
XLA Ops:
  0.6 0.5 %multiply_power_fusion.spread_h = f32[1,128]{1,0:T(1,128)} fusion(), kind=kLoop, calls=%fused_computation | loop fusion | flops 256 | bytes 512 | tf_op jit(solution)/shard_map/pow | solution.py:604
  1.2 43.5 %shard_map.113 = (bf16[6,2048]{1,0:T(8,128)(2,1)}, bf16[3,512]{1,0:T(4,128)(2,1)}) custom-call(s32[3]{0:T(128)} %lengths_ref.1, bf16[6,2048]{1,0:T(8,128)(2,1)} %tokens_h.1, f32[1,2048]{1,0:T(1,128)} %bitcast.1, f32[1,128]{1,0:T(1,128)} %multiply_power_fusion.spread_h, bf16[2048,1024]{1,0:T(8,128)(2,1)} %q_h.1, bf16[2048,512]{1,0:T(8,128)(2,1)} %kv_h.1, ...), custom_call_target="tpu_custom_call" | custom-call | tf_op jit(solution)/shard_map/pallas_call | solution.py:653
  44.7 1.4 %copy.14 = bf16[6,2048]{1,0:T(8,128)(2,1)} copy(bf16[6,2048]{1,0:T(8,128)(2,1)} %get-tuple-element.4) | data formatting | bytes 49152
  46.0 1.3 %copy.15 = bf16[3,512]{1,0:T(4,128)(2,1)} copy(bf16[3,512]{1,0:T(4,128)(2,1)} %get-tuple-element.5) | data formatting | bytes 6144

commit v2 on v1

--- a/solution.py
+++ b/solution.py
@@ -184,6 +184,8 @@
     newkv_v,
     part_v,
     prs_v,
+    side_v,
+    srs_v,
     att_v,
     attall_v,
     gsend_v,
@@ -191,12 +193,14 @@
     own_v,
     hid_v,
     acc_v,
+    heads_v,
     fin_v,
     stat_sem,
     q_sem,
     kvx_sem,
     qa_sem,
     p_sem,
+    s_sem,
     a_sem,
     a_recv,
     g_sem,
@@ -275,6 +279,20 @@
     stat_v[gx] = jnp.where(
         lane < 64, jnp.sum(x, 1, keepdims=True), jnp.sum(x * x, 1, keepdims=True)
     )
+    small[1].wait()
+    spare = lax.broadcasted_iota(jnp.int32, (rp, dx), 0) == rows
+    local_mean = stat_v[gx][:, 0:1] / dx
+    centred = jnp.where(spare, 1.0, x - local_mean)
+    normed_v[...] = (centred * gain_v[...]).astype(BF16)
+
+    qo = own_heads * HEAD_DIM
+    small[3].wait()
+
+    @pl.loop(0, ngx)
+    def _(j):
+        columns = pl.ds(pl.multiple_of(j * qo, qo), qo)
+        qp_v[j] = jnp.dot(normed_v[...], q_v[:, columns], preferred_element_type=F32)
+
     pl.semaphore_wait(barrier, len(offsets))
 
     pending = []
@@ -304,7 +322,12 @@
     for k in range(1, ngx):
         peer = lax.rem(gx + k, ngx)
         send(stat_v.at[gx], stat_v.at[gx], stat_sem.at[0, peer], stat_sem.at[1, gx], at(peer, gy, gz))
-    small[1].wait()
+        send(qp_v.at[peer], qrs_v.at[gx], q_sem.at[0, peer], q_sem.at[1, gx], at(peer, gy, gz))
+    small[4].wait()
+    kvs_v[gx] = jnp.dot(normed_v[...], kv_v[...], preferred_element_type=F32)
+    for k in range(1, ngx):
+        peer = lax.rem(gx + k, ngx)
+        send(kvs_v.at[gx], kvs_v.at[gx], kvx_sem.at[0, peer], kvx_sem.at[1, gx], at(peer, gy, gz))
     small[2].wait()
 
     row = lax.broadcasted_iota(jnp.int32, (rp, middle), 0)
@@ -315,32 +338,19 @@
     cosine = jnp.cos(angle)
     sine = jnp.sin(angle)
 
-    for k in range(1, ngx):
-        peer = lax.rem(gx + k, ngx)
-        arrived(stat_v.at[peer], stat_sem.at[1, peer])
-    totals = stat_v[0]
-    for k in range(1, ngx):
-        totals = totals + stat_v[k]
-    center = totals[:, 0:1] / D
-    spread_sq = totals[:, 64:65] / D - center * center
-    normed_v[...] = ((x_v[...] - center) * lax.rsqrt(spread_sq + epsilon) * gain_v[...]).astype(BF16)
-
-    qo = own_heads * HEAD_DIM
-    small[3].wait()
-
-    @pl.loop(0, ngx)
-    def _(j):
-        columns = pl.ds(pl.multiple_of(j * qo, qo), qo)
-        qp_v[j] = jnp.dot(normed_v[...], q_v[:, columns], preferred_element_type=F32)
-
-    for k in range(1, ngx):
-        peer = lax.rem(gx + k, ngx)
-        send(qp_v.at[peer], qrs_v.at[gx], q_sem.at[0, peer], q_sem.at[1, gx], at(peer, gy, gz))
-    small[4].wait()
-    kvs_v[gx] = jnp.dot(normed_v[...], kv_v[...], preferred_element_type=F32)
-    for k in range(1, ngx):
-        peer = lax.rem(gx + k, ngx)
-        send(kvs_v.at[gx], kvs_v.at[gx], kvx_sem.at[0, peer], kvx_sem.at[1, gx], at(peer, gy, gz))
+    def moments():
+        for k in range(1, ngx):
+            peer = lax.rem(gx + k, ngx)
+            arrived(stat_v.at[peer], stat_sem.at[1, peer])
+        totals = stat_v[0]
+        for k in range(1, ngx):
+            totals = totals + stat_v[k]
+        center = totals[:, 0:1] / D
+        spread_sq = totals[:, 64:65] / D - center * center
+        return center, lax.rsqrt(spread_sq + epsilon)
+
+    def corrected(part, gain_row, source, center):
+        return part + (stat_v[source][:, 0:1] / dx - center) * gain_row
 
     tile = min(512, fb)
 
@@ -364,11 +374,15 @@
             send(gsend_v.at[step], grs_v.at[gx], g_sem.at[0, peer], g_sem.at[1, gx], at(peer, gy, gz))
 
     def gather_query():
-        total = qp_v[gx]
-        for k in range(1, ngx):
+        qrs_v[gx] = qp_v[gx]
+        total = None
+        for k in range(ngx):
             peer = lax.rem(gx + k, ngx)
-            arrived(qrs_v.at[peer], q_sem.at[1, peer])
-            total = total + qrs_v[peer]
+            if k:
+                arrived(qrs_v.at[peer], q_sem.at[1, peer])
+            part = corrected(qrs_v[peer], qrs_v[peer, rows : rows + 1, :], peer, center)
+            total = part if total is None else total + part
+        total = total * inverse
         mine = (gy * ngz + gz) * heads_dev + gx * own_heads
         for h in range(own_heads):
             piece = total[:, h * HEAD_DIM : (h + 1) * HEAD_DIM].astype(BF16)
@@ -387,11 +401,14 @@
     me_owner = gx * ngz + gz
 
     def attend():
-        keyval = kvs_v[gx]
-        for k in range(1, ngx):
+        keyval = None
+        for k in range(ngx):
             peer = lax.rem(gx + k, ngx)
-            arrived(kvs_v.at[peer], kvx_sem.at[1, peer])
-            keyval = keyval + kvs_v[peer]
+            if k:
+                arrived(kvs_v.at[peer], kvx_sem.at[1, peer])
+            part = corrected(kvs_v[peer], kvs_v[peer, rows : rows + 1, :], peer, center)
+            keyval = part if keyval is None else keyval + part
+        keyval = keyval * inverse
         a = keyval[:, :middle]
         b = keyval[:, middle:HEAD_DIM]
         newkv_v[:, :middle] = a * cosine - b * sine
@@ -439,9 +456,17 @@
                 cache_v[s, :, HEAD_DIM:],
                 preferred_element_type=F32,
             )
-        lanes = lax.broadcasted_iota(jnp.int32, (HEADS * rp, 128), 1)
-        part_v[:, :, :HEAD_DIM] = numer.reshape(HEADS, rp, HEAD_DIM)
-        part_v[:, :, HEAD_DIM:] = jnp.where(lanes < 64, top, denom).reshape(HEADS, rp, 128)
+        part_v[...] = numer.reshape(HEADS, rp, HEAD_DIM).astype(BF16)
+        wide = 64 // part_heads
+        lanes = lax.broadcasted_iota(jnp.int32, (owners, rp, 128), 2)
+        top4 = jnp.broadcast_to(top, (HEADS * rp, 128)).reshape(owners, part_heads, rp, 128)
+        denom4 = jnp.broadcast_to(denom, (HEADS * rp, 128)).reshape(owners, part_heads, rp, 128)
+        packed = jnp.zeros((owners, rp, 128), F32)
+        for h in range(part_heads):
+            low = lanes >= h * wide
+            packed = jnp.where(low & (lanes < 64), top4[:, h], packed)
+            packed = jnp.where(lanes >= 64 + h * wide, denom4[:, h], packed)
+        side_v[...] = packed
         for ox, oz in itertools.product(range(ngx), range(ngz)):
             if ox or oz:
                 px, py, pz = shifted(ox, 0, oz)
@@ -453,6 +478,13 @@
                     p_sem.at[1, me_owner],
                     at(px, py, pz),
                 )
+                send(
+                    side_v.at[peer],
+                    srs_v.at[me_owner],
+                    s_sem.at[0, peer],
+                    s_sem.at[1, me_owner],
+                    at(px, py, pz),
+                )
 
     block = (me_owner * part_heads) // heads_dev
     by, bz = block // ngz, lax.rem(block, ngz)
@@ -460,15 +492,27 @@
 
     def combine_parts():
         prs_v[me_owner] = part_v[pl.ds(me_owner * part_heads, part_heads)]
+        srs_v[me_owner] = side_v[me_owner]
         for ox, oz in itertools.product(range(ngx), range(ngz)):
             if ox or oz:
                 px, py, pz = shifted(ox, 0, oz)
                 peer = px * ngz + pz
                 arrived(prs_v.at[peer], p_sem.at[1, peer])
+                arrived(srs_v.at[peer], s_sem.at[1, peer])
+        wide = 64 // part_heads
+
+        def column(o, start):
+            return jnp.stack(
+                [
+                    srs_v[o, :, start + h * wide : start + h * wide + 1]
+                    for h in range(part_heads)
+                ]
+            )
+
         rot = rot_v[pl.ds(me_owner * part_heads, part_heads)]
         newkv = newkv_v[...].astype(BF16).astype(F32)
         own = jnp.sum(rot * newkv[:, :HEAD_DIM], 2, keepdims=True) * scale
-        tops = [prs_v[o, :, :, HEAD_DIM : HEAD_DIM + 1] for o in range(owners)]
+        tops = [column(o, 0) for o in range(owners)]
         top = own
         for t in tops:
             top = jnp.maximum(top, t)
@@ -477,8 +521,8 @@
         denom = weight
         for o in range(owners):
             factor = jnp.exp(tops[o] - top)
-            numer = numer + factor * prs_v[o, :, :, :HEAD_DIM]
-            denom = denom + factor * prs_v[o, :, :, HEAD_DIM + 64 : HEAD_DIM + 65]
+            numer = numer + factor * prs_v[o].astype(F32)
+            denom = denom + factor * column(o, 64)
         rowid = lax.broadcasted_iota(jnp.int32, (part_heads, rp, HEAD_DIM), 1)
         mine = (rowid >= first) & (rowid < first + seq_dev)
         att_v[...] = jnp.where(mine, numer / denom, 0.0).astype(BF16)
@@ -526,16 +570,17 @@
         mixed_heads = jnp.concatenate(pieces, 1)
         small[6].wait()
         ct = min(512, dx)
-        normed_v[:, :qd] = mixed_heads
+        heads_v[...] = mixed_heads
 
         @pl.loop(0, dx // ct)
         def _(n):
             columns = pl.ds(pl.multiple_of(n * ct, ct), ct)
-            acc_v[:, columns] = jnp.dot(
-                normed_v[:, :qd], out_v[:, columns], preferred_element_type=F32
+            acc_v[:, columns] += jnp.dot(
+                heads_v[...], out_v[:, columns], preferred_element_type=F32
             )
 
     gate_up(0)
+    center, inverse = moments()
     gather_query()
     gate_up(1)
     attend()
@@ -544,47 +589,75 @@
     for step in range(3, ngx):
         gate_up(step)
 
-    both = own_v[...]
-    for k in range(1, ngx):
+    g = u = None
+    for k in range(ngx):
         peer = lax.rem(gx + k, ngx)
-        arrived(grs_v.at[peer], g_sem.at[1, peer])
-        both = both + grs_v[peer].astype(F32)
-    g = both[:rp]
-    u = both[rp:]
+        if k:
+            arrived(grs_v.at[peer], g_sem.at[1, peer])
+            both = grs_v[peer].astype(F32)
+        else:
+            both = own_v[...]
+        g_part = corrected(both[:rp], both[rows : rows + 1], peer, center)
+        u_part = corrected(both[rp:], both[rp + rows : rp + rows + 1], peer, center)
+        g = g_part if g is None else g + g_part
+        u = u_part if u is None else u + u_part
+    g = g * inverse
+    u = u * inverse
     hid_v[gx] = (g / (1.0 + jnp.exp(-g)) * u).astype(BF16)
     for k in range(1, ngx):
         peer = lax.rem(gx + k, ngx)
         send(hid_v.at[gx], hid_v.at[gx], h_sem.at[0, peer], h_sem.at[1, gx], at(peer, gy, gz))
 
+    spot = gy * ngz + gz
+    ct = min(512, dx // 2)
+    half = dx // 2
+    peers = [o for o in itertools.product(range(ngy), range(ngz)) if any(o)]
+
+    def down_product(step, low, high):
+        source = lax.rem(gx + step, ngx)
+
+        @pl.loop(low // ct, high // ct)
+        def _(n):
+            columns = pl.ds(pl.multiple_of(n * ct, ct), ct)
+            product = jnp.dot(
+                hid_v[source], down_v[step, :, columns], preferred_element_type=F32
+            )
+            if step:
+                acc_v[:, columns] += product
+            else:
+                acc_v[:, columns] = product
+
+    down_copy(0).wait()
+    down_product(0, 0, dx)
     out_product()
-    spot = gy * ngz + gz
-    ct = min(512, dx)
-    for step in range(ngx):
+    for step in range(1, ngx):
         source = lax.rem(gx + step, ngx)
         down_copy(step).wait()
-        if step:
-            arrived(hid_v.at[source], h_sem.at[1, source])
-
-        @pl.loop(0, dx // ct)
-        def _(n):
-            columns = pl.ds(pl.multiple_of(n * ct, ct), ct)
-            acc_v[:, columns] += jnp.dot(
-                hid_v[source], down_v[step, :, columns], preferred_element_type=F32
-            )
-
-    fin_v[spot] = acc_v[...].astype(BF16)
-    peers = [o for o in itertools.product(range(ngy), range(ngz)) if any(o)]
-    for oy, oz in peers:
-        px, py, pz = shifted(0, oy, oz)
-        peer = py * ngz + pz
-        send(fin_v.at[spot], fin_v.at[spot], f_sem.at[0, peer], f_sem.at[1, spot], at(px, py, pz))
-    total = x_v[...] + acc_v[...]
-    for oy, oz in peers:
-        px, py, pz = shifted(0, oy, oz)
-        peer = py * ngz + pz
-        arrived(fin_v.at[peer], f_sem.at[1, peer])
-        total = total + fin_v[peer].astype(F32)
-    mixed_ref[...] = total[:rows].astype(BF16)
+        arrived(hid_v.at[source], h_sem.at[1, source])
+        if step < ngx - 1:
+            down_product(step, 0, dx)
+    for part in range(2):
+        down_product(ngx - 1, part * half, (part + 1) * half)
+        fin_v[part, spot] = acc_v[:, part * half : (part + 1) * half].astype(BF16)
+        for oy, oz in peers:
+            px, py, pz = shifted(0, oy, oz)
+            peer = py * ngz + pz
+            send(
+                fin_v.at[part, spot],
+                fin_v.at[part, spot],
+                f_sem.at[0, part, peer],
+                f_sem.at[1, part, spot],
+                at(px, py, pz),
+            )
+    for part in range(2):
+        columns = slice(part * half, (part + 1) * half)
+        total = x_v[:, columns] + acc_v[:, columns]
+        for oy, oz in peers:
+            px, py, pz = shifted(0, oy, oz)
+            peer = py * ngz + pz
+            arrived(fin_v.at[part, peer], f_sem.at[1, part, peer])
+            total = total + fin_v[part, peer].astype(F32)
+        mixed_ref[:, columns] = total[:rows].astype(BF16)
     for copy in pending:
         copy.wait_send()
 
@@ -593,7 +666,7 @@
     (tokens, gain, qw, kvw, outw, gatew, upw, downw, cache, lengths) = args
     ngx, ngy, ngz = sizes
     rows, dx = tokens.shape
-    rp = -(-rows // 8) * 8
+    rp = (rows // 8 + 1) * 8
     qd = qw.shape[1]
     fb = gatew.shape[1] // ngx
     own_heads = qd // HEAD_DIM // ngx
@@ -628,8 +701,10 @@
         vm((HEADS, rp, HEAD_DIM), BF16),
         vm((HEADS, rp, HEAD_DIM), F32),
         vm((rp, 2 * HEAD_DIM), F32),
-        vm((HEADS, rp, HEAD_DIM + 128), F32),
-        vm((owners, part_heads, rp, HEAD_DIM + 128), F32),
+        vm((HEADS, rp, HEAD_DIM), BF16),
+        vm((owners, part_heads, rp, HEAD_DIM), BF16),
+        vm((owners, rp, 128), F32),
+        vm((owners, rp, 128), F32),
         vm((part_heads, rp, HEAD_DIM), BF16),
         vm((ngy, heads_dev // part_heads, part_heads, rp, HEAD_DIM), BF16),
         vm((ngx - 1, 2 * rp, fb), BF16),
@@ -637,39 +712,43 @@
         vm((2 * rp, fb), F32),
         vm((ngx, rp, fb), BF16),
         vm((rp, dx), F32),
-        vm((ngy * ngz, rp, dx), BF16),
+        vm((rp, qd), BF16),
+        vm((2, ngy * ngz, rp, dx // 2), BF16),
         dma((2, ngx)),
         dma((2, ngx)),
         dma((2, ngx)),
         dma((2, ngx, ngy, ngz)),
         dma((2, owners)),
+        dma((2, owners)),
         dma((ngx,)),
         dma((ngy, heads_dev // part_heads)),
         dma((2, ngx)),
         dma((2, ngx)),
-        dma((2, ngy * ngz)),
+        dma((2, 2, ngy * ngz)),
     ]
     anywhere = pl.BlockSpec(memory_space=pl.ANY)
     return pl.pallas_call(
         functools.partial(kernel, (ngx, ngy, ngz, rows, rp)),
         out_shape=(
-            jax.ShapeDtypeStruct(tokens.shape, BF16),
-            jax.ShapeDtypeStruct((cache.shape[0], 2 * HEAD_DIM), BF16),
+            pltpu.VMEM(tokens.shape, BF16),
+            pltpu.VMEM((cache.shape[0], 2 * HEAD_DIM), BF16),
         ),
         in_specs=[pl.BlockSpec(memory_space=pltpu.SMEM)] + [anywhere] * 10,
         out_specs=(pl.BlockSpec(memory_space=pltpu.VMEM),) * 2,
         scratch_shapes=scratch,
         compiler_params=pltpu.CompilerParams(
-            collective_id=0, has_side_effects=True, vmem_limit_bytes=67043328
+            collective_id=0, has_side_effects=True, vmem_limit_bytes=61 * 2**20
         ),
     )(lengths, tokens, gain.reshape(1, dx), spread, qw, kvw, cache, gatew, upw, outw, downw)
 
 
-def fits(sizes, q_dev, ff_dev, weight_bytes):
+def fits(sizes, d_dev, q_dev, ff_dev, weight_bytes):
     ngx, ngy, ngz = sizes
     heads_dev = q_dev // HEAD_DIM
     return (
         ngx >= 3
+        and HEADS // (ngx * ngz) in (1, 2, 4)
+        and d_dev % 1024 == 0
         and heads_dev % ngx == 0
         and HEADS % (ngx * ngz) == 0
         and heads_dev % (HEADS // (ngx * ngz)) == 0
@@ -680,7 +759,7 @@
 
 def choose(sizes, *args):
     held = sum(a.size * a.dtype.itemsize for a in args[2:9])
-    if fits(sizes, args[2].shape[1], args[5].shape[1], held):
+    if fits(sizes, args[0].shape[1], args[2].shape[1], args[5].shape[1], held):
         return fused(sizes, *args)
     return body(*args)
 

time: 47.5 us -> 42.6 us (0.90)
  Pallas kernels: 43.5 us -> 40.1 us
  local copies, waits for them, and re-layouts: 2.65 us -> 1.21 us
    pallas_call x1, Pallas kernels: 43.5 us -> 40.1 us  [fused(): pl.pallas_call(functools.partial(kernel, (ngx, ngy, ngz, rows, rp)), out_...]
    unnamed x2, local copies, waits for them, and re-layouts: 2.65 us -> 1.21 us
where the time goes in v2:
time: 42.6 us; the launch traced here: 42.5 us
  Pallas kernels  40.1 us (94%)
  local copies, waits for them, and re-layouts  1.21 us (3%)
  between operations  0.64 us (2%)
  other arithmetic  0.53 us (1%)
    pallas_call x1, Pallas kernels, fused(): pl.pallas_call(functools.partial(kernel, (ngx, ngy, ngz, rows, rp)), out_...  40.1 us
    unnamed x2, local copies, waits for them, and re-layouts  1.21 us

profile of v2, /device:TPU:0, one launch (start us, length us, event | category | flops | bytes accessed | tf_op | source)
XLA Modules:
  0.0 42.5 jit_solution(1594806637061624501)
XLA Ops:
  0.6 0.5 %multiply_power_fusion.spread_h = f32[1,128]{1,0:T(1,128)} fusion(), kind=kLoop, calls=%fused_computation | loop fusion | flops 256 | bytes 512 | tf_op jit(solution)/shard_map/pow | solution.py:677
  1.2 40.1 %shard_map.113 = (bf16[6,2048]{1,0:T(8,128)(2,1)S(1)}, bf16[3,512]{1,0:T(4,128)(2,1)S(1)}) custom-call(s32[3]{0:T(128)} %lengths_ref.1, bf16[6,2048]{1,0:T(8,128)(2,1)} %tokens_h.1, f32[1,2048]{1,0:T(1,128)} %bitcast.1, f32[1,128]{1,0:T(1,128)} %multiply_power_fusion.spread_h, bf16[2048,1024]{1,0:T(8,128)(2,1)} %q_h.1, bf16[2048,512]{1,0:T(8,128)(2,1)} %kv_h.1, ...), custom_call_target="tpu_custom_call" | custom-call | tf_op jit(solution)/shard_map/pallas_call | solution.py:730
  41.2 0.6 %copy.14 = bf16[6,2048]{1,0:T(8,128)(2,1)} copy(bf16[6,2048]{1,0:T(8,128)(2,1)S(1)} %get-tuple-element.2) | data formatting | bytes 49152
  41.9 0.6 %copy.15 = bf16[3,512]{1,0:T(4,128)(2,1)} copy(bf16[3,512]{1,0:T(4,128)(2,1)S(1)} %get-tuple-element.3) | data formatting | bytes 6144

commit v3 on v2

--- a/solution.py
+++ b/solution.py
@@ -3,6 +3,7 @@
 
 import jax
 import jax.numpy as jnp
+import numpy as np
 from jax import lax
 from jax.experimental import pallas as pl
 from jax.experimental.pallas import tpu as pltpu
@@ -250,6 +251,18 @@
         picked = pl.ds(pl.multiple_of(block * fb, fb), fb)
         return pltpu.make_async_copy(down_h.at[picked], down_v.at[step], down_sem.at[step])
 
+    offsets = [o for o in itertools.product(range(ngx), range(ngy), range(ngz)) if any(o)]
+
+    def shifted(ox, oy, oz):
+        return lax.rem(gx + ox, ngx), lax.rem(gy + oy, ngy), lax.rem(gz + oz, ngz)
+
+    def at(px, py, pz):
+        return {"gx": px, "gy": py, "gz": pz}
+
+    barrier = pltpu.get_barrier_semaphore()
+    for offset in offsets:
+        pl.semaphore_signal(barrier, inc=1, device_id=at(*shifted(*offset)), device_id_type=MESH)
+
     for copy in small[:6]:
         copy.start()
     for step in range(ngx):
@@ -258,18 +271,6 @@
     small[6].start()
     for step in range(ngx):
         down_copy(step).start()
-
-    offsets = [o for o in itertools.product(range(ngx), range(ngy), range(ngz)) if any(o)]
-
-    def shifted(ox, oy, oz):
-        return lax.rem(gx + ox, ngx), lax.rem(gy + oy, ngy), lax.rem(gz + oz, ngz)
-
-    def at(px, py, pz):
-        return {"gx": px, "gy": py, "gz": pz}
-
-    barrier = pltpu.get_barrier_semaphore()
-    for offset in offsets:
-        pl.semaphore_signal(barrier, inc=1, device_id=at(*shifted(*offset)), device_id_type=MESH)
 
     small[0].wait()
     x_v[...] = jnp.zeros_like(x_v)
@@ -551,7 +552,7 @@
                     copy.start()
                     copy.wait_send()
 
-    def out_product():
+    def gather_heads():
         for sy in range(ngy):
             for sl in range(heads_dev // part_heads):
                 owner = (gy * ngz + gz) * (heads_dev // part_heads) + sl
@@ -569,10 +570,10 @@
             pieces.append(total.astype(BF16))
         mixed_heads = jnp.concatenate(pieces, 1)
         small[6].wait()
-        ct = min(512, dx)
         heads_v[...] = mixed_heads
 
-        @pl.loop(0, dx // ct)
+    def out_product(low, high):
+        @pl.loop(low // ct, high // ct)
         def _(n):
             columns = pl.ds(pl.multiple_of(n * ct, ct), ct)
             acc_v[:, columns] += jnp.dot(
@@ -582,12 +583,10 @@
     gate_up(0)
     center, inverse = moments()
     gather_query()
-    gate_up(1)
+    for step in range(1, ngx - 1):
+        gate_up(step)
     attend()
-    gate_up(2)
-    combine_parts()
-    for step in range(3, ngx):
-        gate_up(step)
+    gate_up(ngx - 1)
 
     g = u = None
     for k in range(ngx):
@@ -608,6 +607,7 @@
         peer = lax.rem(gx + k, ngx)
         send(hid_v.at[gx], hid_v.at[gx], h_sem.at[0, peer], h_sem.at[1, gx], at(peer, gy, gz))
 
+    combine_parts()
     spot = gy * ngz + gz
     ct = min(512, dx // 2)
     half = dx // 2
@@ -627,17 +627,15 @@
             else:
                 acc_v[:, columns] = product
 
-    down_copy(0).wait()
-    down_product(0, 0, dx)
-    out_product()
-    for step in range(1, ngx):
+    for step in range(ngx):
         source = lax.rem(gx + step, ngx)
         down_copy(step).wait()
-        arrived(hid_v.at[source], h_sem.at[1, source])
-        if step < ngx - 1:
-            down_product(step, 0, dx)
+        if step:
+            arrived(hid_v.at[source], h_sem.at[1, source])
+        down_product(step, 0, dx)
+    gather_heads()
     for part in range(2):
-        down_product(ngx - 1, part * half, (part + 1) * half)
+        out_product(part * half, (part + 1) * half)
         fin_v[part, spot] = acc_v[:, part * half : (part + 1) * half].astype(BF16)
         for oy, oz in peers:
             px, py, pz = shifted(0, oy, oz)
@@ -674,7 +672,9 @@
     owners = ngx * ngz
     part_heads = HEADS // owners
     middle = HEAD_DIM // 2
-    spread = (rotary_base ** (-jnp.arange(middle, dtype=F32) / middle)).reshape(1, middle)
+    spread = np.power(
+        np.float32(rotary_base), -np.arange(middle, dtype=np.float32) / np.float32(middle)
+    ).reshape(1, middle)
     dma = pltpu.SemaphoreType.DMA
     vm = pltpu.VMEM
     scratch = [

time: 42.6 us -> 39.1 us (0.918)
  Pallas kernels: 40.1 us -> 37.1 us
  other arithmetic: 0.53 us -> 0 us
    pallas_call x1, Pallas kernels: 40.1 us -> 37.1 us  [fused(): pl.pallas_call(functools.partial(kernel, (ngx, ngy, ngz, rows, rp)), out_...]
    pow x1 -> x0, other arithmetic: 0.53 us -> none  [fused(): rotary_base ** (-jnp.arange(middle, dtype=F32) / middle)]
where the time goes in v3:
time: 39.1 us; the launch traced here: 39 us
  Pallas kernels  37.1 us (95%)
  local copies, waits for them, and re-layouts  1.21 us (3%)
  between operations  0.64 us (2%)
    pallas_call x1, Pallas kernels, fused(): pl.pallas_call(functools.partial(kernel, (ngx, ngy, ngz, rows, rp)), out_...  37.1 us
    unnamed x2, local copies, waits for them, and re-layouts  1.21 us

profile of v3, /device:TPU:0, one launch (start us, length us, event | category | flops | bytes accessed | tf_op | source)
XLA Modules:
  0.0 39.0 jit_solution(17381763781235043461)
XLA Ops:
  0.6 37.1 %shard_map.122 = (bf16[6,2048]{1,0:T(8,128)(2,1)S(1)}, bf16[3,512]{1,0:T(4,128)(2,1)S(1)}) custom-call(s32[3]{0:T(128)} %lengths_ref.1, bf16[6,2048]{1,0:T(8,128)(2,1)} %tokens_h.1, f32[1,2048]{1,0:T(1,128)} %bitcast.1, f32[1,128]{1,0:T(1,128)} %constant.2.clone.spread_h, bf16[2048,1024]{1,0:T(8,128)(2,1)} %q_h.1, bf16[2048,512]{1,0:T(8,128)(2,1)} %kv_h.1, ...), custom_call_target="tpu_custom_call" | custom-call | tf_op jit(solution)/shard_map/pallas_call | solution.py:730
  37.8 0.6 %copy.15 = bf16[6,2048]{1,0:T(8,128)(2,1)} copy(bf16[6,2048]{1,0:T(8,128)(2,1)S(1)} %get-tuple-element.2) | data formatting | bytes 49152
  38.4 0.6 %copy.16 = bf16[3,512]{1,0:T(4,128)(2,1)} copy(bf16[3,512]{1,0:T(4,128)(2,1)S(1)} %get-tuple-element.3) | data formatting | bytes 6144

commit v4 on v3

--- a/solution.py
+++ b/solution.py
@@ -265,12 +265,8 @@
 
     for copy in small[:6]:
         copy.start()
-    for step in range(ngx):
-        for copy in gu_copies(step):
-            copy.start()
-    small[6].start()
-    for step in range(ngx):
-        down_copy(step).start()
+    for copy in gu_copies(0):
+        copy.start()
 
     small[0].wait()
     x_v[...] = jnp.zeros_like(x_v)
@@ -288,6 +284,8 @@
 
     qo = own_heads * HEAD_DIM
     small[3].wait()
+    for copy in gu_copies(1):
+        copy.start()
 
     @pl.loop(0, ngx)
     def _(j):
@@ -358,6 +356,13 @@
     def gate_up(step):
         for copy in gu_copies(step):
             copy.wait()
+        if step + 2 < ngx:
+            for copy in gu_copies(step + 2):
+                copy.start()
+        elif step + 2 == ngx:
+            for later in range(ngx):
+                down_copy(later).start()
+            small[6].start()
 
         @pl.loop(0, fb // tile)
         def _(n):

time: 39.1 us -> 33.9 us (0.87)
  Pallas kernels: 37.1 us -> 31.9 us
    pallas_call x1, Pallas kernels: 37.1 us -> 31.9 us  [fused(): pl.pallas_call(functools.partial(kernel, (ngx, ngy, ngz, rows, rp)), out_...]
where the time goes in v4:
time: 33.9 us; the launch traced here: 33.8 us
  Pallas kernels  31.9 us (94%)
  local copies, waits for them, and re-layouts  1.21 us (4%)
  between operations  0.64 us (2%)
    pallas_call x1, Pallas kernels, fused(): pl.pallas_call(functools.partial(kernel, (ngx, ngy, ngz, rows, rp)), out_...  31.9 us
    unnamed x2, local copies, waits for them, and re-layouts  1.21 us

profile of v4, /device:TPU:0, one launch (start us, length us, event | category | flops | bytes accessed | tf_op | source)
XLA Modules:
  0.0 33.8 jit_solution(5096771554503869248)
XLA Ops:
  0.6 31.9 %shard_map.122 = (bf16[6,2048]{1,0:T(8,128)(2,1)S(1)}, bf16[3,512]{1,0:T(4,128)(2,1)S(1)}) custom-call(s32[3]{0:T(128)} %lengths_ref.1, bf16[6,2048]{1,0:T(8,128)(2,1)} %tokens_h.1, f32[1,2048]{1,0:T(1,128)} %bitcast.1, f32[1,128]{1,0:T(1,128)} %constant.2.clone.spread_h, bf16[2048,1024]{1,0:T(8,128)(2,1)} %q_h.1, bf16[2048,512]{1,0:T(8,128)(2,1)} %kv_h.1, ...), custom_call_target="tpu_custom_call" | custom-call | tf_op jit(solution)/shard_map/pallas_call | solution.py:735
  32.6 0.6 %copy.15 = bf16[6,2048]{1,0:T(8,128)(2,1)} copy(bf16[6,2048]{1,0:T(8,128)(2,1)S(1)} %get-tuple-element.2) | data formatting | bytes 49152
  33.2 0.6 %copy.16 = bf16[3,512]{1,0:T(4,128)(2,1)} copy(bf16[3,512]{1,0:T(4,128)(2,1)S(1)} %get-tuple-element.3) | data formatting | bytes 6144
